TPU v7x, 32 devices: a whole 2x2x4 slice. The times are simulated.
32 devices in a mesh: req: 4 (over z), head: 4 (over y, x), blk: 2 (over core).
Axes of the slice: x: 2, y: 2, z: 4, core: 2. Of those that a mesh axis runs over, the one named last changes fastest.
Arguments:
- group_rows: bfloat16 [8, 256, 2048], P(None, 'req', ('head', 'blk')), may hold values from -6 to 6
- slot_request: int32 [8], replicated, may hold values from 0 to 7, each once
- cache_len: int32 [8], replicated, may hold values from 1 to 512, as said below
- group_len: int32 [8], replicated, may hold values from 1 to 256, as said below
- attn_cache: bfloat16 [2, 8, 512, 2048], P(None, 'req', None, ('head', 'blk')), as said below
- hand_cache: bfloat16 [2, 2, 8, 512, 2048], P('blk', None, None, 'req', 'head'), may hold values from -6 to 6
- query_weight: bfloat16 [2048, 2048], P(None, ('head', 'blk')), may hold values from -0.125 to 0.125
- key_weight: bfloat16 [2048, 2048], P(None, ('head', 'blk')), may hold values from -0.125 to 0.125
- value_weight: bfloat16 [2048, 2048], P(None, ('head', 'blk')), may hold values from -0.125 to 0.125
- out_weight: bfloat16 [2048, 2048], P(('head', 'blk')), may hold values from -0.125 to 0.125
- query_gain: float32 [2048], P(('head', 'blk')), may hold values from 0.5 to 1.5
- key_gain: float32 [2048], P(('head', 'blk')), may hold values from 0.5 to 1.5
- attn_gain: float32 [2048], replicated, may hold values from 0.1 to 1.9
- mlp_gain: float32 [2048], replicated, may hold values from 0.1 to 1.9
- gate_weight: bfloat16 [2048, 4096], P(None, ('head', 'blk')), may hold values from -0.125 to 0.125
- up_weight: bfloat16 [2048, 4096], P(None, ('head', 'blk')), may hold values from -0.125 to 0.125
- down_weight: bfloat16 [4096, 2048], P(('head', 'blk')), may hold values from -0.09375 to 0.09375
Outputs:
- layer_out: bfloat16 [8, 256, 2048], P(None, 'req', ('head', 'blk'))
- relaid: bfloat16 [2, 2, 8, 512, 2048], P('blk', None, 'req', None, 'head')
Inputs may be any that keep to these rules, and one draw needn't show every extreme that they name: `cache_len`: some request has exactly 512 cached tokens. `group_len`: some request has exactly 256 valid new tokens. `attn_cache`: entry s along the request dimension belongs to request slot_request[s]; positions from cache_len of that request on are not read.
All inputs are finite; a program needn't handle non-finite values.
Results may differ from a plain program's by a relative error of at most 0.009.
The roundings to bfloat16 on the way count: a program that leaves them out, or rounds other values in their place, can miss the bound.
Values may be sent and summed in bfloat16 or wider, within the bound.
A program may use at most 128 MiB of HBM per device.

v0:
```python
import jax
import jax.numpy as jnp
from jax import lax
from jax.sharding import PartitionSpec as P

HD = 128


EPSILON = 1e-06
ROPE_BASE = 500000.0


def rotate(values, places):
    half_dim = values.shape[-1] // 2
    frequency = ROPE_BASE ** (-(jnp.arange(half_dim, dtype=jnp.float32) * 2.0 / values.shape[-1]))
    angles = places[..., None].astype(jnp.float32) * frequency
    cosine_part = jnp.cos(angles)[..., None, :]
    sine_part = jnp.sin(angles)[..., None, :]
    first_half = values[..., :half_dim]
    second_half = values[..., half_dim:]
    return jnp.concatenate(
        [
            first_half * cosine_part - second_half * sine_part,
            second_half * cosine_part + first_half * sine_part,
        ],
        axis=-1,
    )


def send_home(blocks, inverse):
    received = lax.all_to_all(blocks, "req", split_axis=1, concat_axis=0, tiled=True)
    return jnp.take(received, inverse, axis=0)


def on_device(
    group_rows,
    slot_request,
    cache_len,
    group_len,
    attn_cache,
    hand_cache,
    query_weight,
    key_weight,
    value_weight,
    out_weight,
    query_gain,
    key_gain,
    attn_gain,
    mlp_gain,
    gate_weight,
    up_weight,
    down_weight,
):
    slot_total = slot_request.shape[0]
    slot_count = slot_total // lax.axis_size("req")
    first_slot = lax.axis_index("req") * slot_count
    own_requests = lax.dynamic_slice_in_dim(slot_request, first_slot, slot_count)
    cached = jnp.take(cache_len, own_requests)
    group_valid = jnp.take(group_len, own_requests)
    inverse = (
        jnp.zeros_like(slot_request).at[slot_request].set(jnp.arange(slot_total, dtype=jnp.int32))
    )
    reordered = jnp.take(hand_cache, slot_request, axis=2)
    relaid = lax.all_to_all(reordered, "req", split_axis=2, concat_axis=3, tiled=True)
    local_x = lax.all_to_all(
        jnp.take(group_rows, slot_request, axis=0), "req", split_axis=0, concat_axis=1, tiled=True
    )
    tokens = local_x.shape[1]
    row_width = local_x.shape[2]
    model_width = row_width * lax.axis_size(("head", "blk"))
    feature_start = lax.axis_index(("head", "blk")) * row_width
    full_x = lax.all_gather(local_x, ("head", "blk"), axis=2, tiled=True)
    rows_x = full_x.reshape(-1, model_width)
    queries = jnp.dot(rows_x, query_weight, preferred_element_type=jnp.float32)
    keys_new = jnp.dot(rows_x, key_weight, preferred_element_type=jnp.float32)
    values_new = jnp.dot(rows_x, value_weight, preferred_element_type=jnp.float32)
    square_sums = lax.psum(
        (jnp.sum(queries * queries, axis=-1), jnp.sum(keys_new * keys_new, axis=-1)),
        ("head", "blk"),
    )
    queries = queries * lax.rsqrt(square_sums[0] / model_width + EPSILON)[:, None] * query_gain
    keys_new = keys_new * lax.rsqrt(square_sums[1] / model_width + EPSILON)[:, None] * key_gain
    heads_here = row_width // HD
    places = cached[:, None] + jnp.arange(tokens, dtype=jnp.int32)[None, :]
    queries = rotate(queries.reshape(slot_count, tokens, heads_here, HD), places).astype(
        jnp.bfloat16
    )
    keys_new = rotate(keys_new.reshape(slot_count, tokens, heads_here, HD), places).astype(
        jnp.bfloat16
    )
    values_new = values_new.astype(jnp.bfloat16).reshape(slot_count, tokens, heads_here, HD)
    keys_old = attn_cache[0].reshape(slot_count, -1, heads_here, HD)
    values_old = attn_cache[1].reshape(slot_count, -1, heads_here, HD)
    score_scale = 1.0 / HD**0.5
    span_old = keys_old.shape[1]
    old_scores = (
        jnp.einsum("sthd,sjhd->shtj", queries, keys_old, preferred_element_type=jnp.float32)
        * score_scale
    )
    new_scores = (
        jnp.einsum("sthd,sjhd->shtj", queries, keys_new, preferred_element_type=jnp.float32)
        * score_scale
    )
    old_mask = (jnp.arange(span_old)[None, :] < cached[:, None])[:, None, None, :]
    columns = jnp.arange(tokens)
    new_mask = (columns[None, None, :] <= columns[None, :, None]) & (
        columns[None, None, :] < group_valid[:, None, None]
    )
    new_mask = new_mask[:, None, :, :]
    scores = jnp.concatenate(
        [jnp.where(old_mask, old_scores, -1e30), jnp.where(new_mask, new_scores, -1e30)], axis=-1
    )
    row_top = jnp.max(scores, axis=-1, keepdims=True)
    weights = jnp.exp(scores - row_top)
    weights = (weights / jnp.sum(weights, axis=-1, keepdims=True)).astype(jnp.bfloat16)
    stacked = jnp.concatenate([values_old, values_new], axis=1)
    attended = jnp.einsum("shtj,sjhd->sthd", weights, stacked, preferred_element_type=jnp.float32)
    attended = attended.astype(jnp.bfloat16).reshape(-1, row_width)
    partial_value = jnp.dot(attended, out_weight, preferred_element_type=jnp.float32)
    totals = lax.psum(partial_value, ("head", "blk"))
    normed = (
        totals * lax.rsqrt(jnp.mean(totals * totals, axis=-1, keepdims=True) + EPSILON) * attn_gain
    )
    state_full = (rows_x.astype(jnp.float32) + normed).astype(jnp.bfloat16)
    state_part = lax.dynamic_slice_in_dim(state_full, feature_start, row_width, 1)
    gate_act = jnp.dot(state_full, gate_weight, preferred_element_type=jnp.float32)
    up_act = jnp.dot(state_full, up_weight, preferred_element_type=jnp.float32)
    inner = (jax.nn.silu(gate_act) * up_act).astype(jnp.bfloat16)
    down_sum = jnp.dot(inner, down_weight, preferred_element_type=jnp.float32)
    down_share = lax.psum_scatter(down_sum, ("head", "blk"), scatter_dimension=1, tiled=True)
    down_power = lax.psum(jnp.sum(down_share * down_share, axis=-1), ("head", "blk"))
    mgain_part = lax.dynamic_slice_in_dim(mlp_gain, feature_start, row_width)
    result = (
        state_part.astype(jnp.float32)
        + down_share * lax.rsqrt(down_power / model_width + EPSILON)[:, None] * mgain_part
    ).astype(jnp.bfloat16)
    layer_out = send_home(result.reshape(slot_count, tokens, row_width), inverse)
    return (layer_out, relaid)


def solution(mesh):
    in_specs = (
        P(None, "req", ("head", "blk")),
        P(),
        P(),
        P(),
        P(None, "req", None, ("head", "blk")),
        P("blk", None, None, "req", "head"),
        P(None, ("head", "blk")),
        P(None, ("head", "blk")),
        P(None, ("head", "blk")),
        P(("head", "blk"), None),
        P(("head", "blk")),
        P(("head", "blk")),
        P(),
        P(),
        P(None, ("head", "blk")),
        P(None, ("head", "blk")),
        P(("head", "blk"), None),
    )
    out_specs = (P(None, "req", ("head", "blk")), P("blk", None, "req", None, "head"))
    return jax.shard_map(
        on_device, mesh=mesh, in_specs=in_specs, out_specs=out_specs, check_vma=False
    )
```

profile of v0, /device:TPU:0, one launch (start us, length us, event | category | flops | bytes accessed | tf_op | source)
XLA Modules:
  0.0 288.7 jit_solution(8035457051612961432)
XLA Ops:
  7.3 0.8 compare_select_fusion.2
  8.1 0.7 compare_and_fusion.2
  8.7 1.5 gather_fusion.1
  10.2 0.1 broadcast_select_fusion.1
  10.3 15.0 %all_to_all.54 = bf16[8,64,256]{2,1,0:T(8,128)(2,1)S(1)} all-to-all(bf16[8,64,256]{2,1,0:T(8,128)(2,1)S(1)} %broadcast_select_fusion.1), channel_id=1, replica_groups=mesh['req'=4,'head'=4,'blk'=2] {'req'}, dimensions={0} | all-to-all | bytes 524288 | tf_op jit(solution)/shard_map/all_to_all | solution.py:65
  25.3 0.7 copy.53
  26.1 0.1 compare_select_fusion.1
  26.2 0.6 gather_fusion.2
  26.9 0.6 gather_fusion.3
  27.5 1.3 fusion.25
  28.8 1.0 copy.76
  29.8 1.0 copy.54
  30.9 0.1 broadcast_select_fusion.3
  30.9 0.1 iota_compare_fusion.2
  31.0 0.1 add_convert_fusion.4
  31.1 0.1 iota_compare_fusion.1
  31.2 1.7 multiply_cosine_fusion
  33.0 20.6 %all-gather.2.cloned.1.call-done = bf16[2,256,2048]{2,1,0:T(8,128)(2,1)} async-done(((bf16[2,256,256]{2,1,0:T(8,128)(2,1)}), bf16[2,256,2048]{2,1,0:T(8,128)(2,1)}) %all-gather.2.cloned.1.call-update) | async-done | bytes 2097168 | tf_op jit(solution)/shard_map/all_gather | solution.py:72
  53.6 2.8 multiply_reduce_fusion.2
  56.3 2.8 multiply_reduce_fusion.3
  59.1 13.1 %all-reduce = (f32[512]{0:T(512)S(1)}, f32[512]{0:T(512)S(1)}) all-reduce(f32[512]{0:T(512)S(1)} %get-tuple-element.22, f32[512]{0:T(512)S(1)} %get-tuple-element.24), channel_id=1, replica_groups=mesh['req'=4,'head'=4,'blk'=2] {'head','blk'}, use_global_device_ids=true, to_apply=%region_3.6 | all-reduce | flops 1024 | bytes 8192 | tf_op jit(solution)/shard_map/psum | solution.py:77
  72.2 0.8 multiply_multiply_fusion
  73.0 0.3 reshape.220
  73.4 1.0 fusion.27
  74.3 1.1 copy.77
  75.5 1.1 copy.78
  76.7 1.9 multiply_multiply_fusion.1
  78.6 2.2 reshape.152
  80.8 2.0 fusion.26
  82.8 2.0 copy.74
  84.7 1.9 copy.75
  86.7 3.3 %convolution_convert_fusion = bf16[512,256]{1,0:T(8,128)(2,1)} fusion(bf16[512,2048]{1,0:T(8,128)(2,1)} %bitcast.50, bf16[2048,256]{1,0:T(8,128)(2,1)} %param.29), kind=kOutput, calls=%fused_computation.20 | convolution fusion | flops 537001984 | bytes 3407872 | tf_op jit(solution)/shard_map/dot_general | solution.py:76
  90.0 1.7 reshape.151
  91.7 1.8 copy.55
  93.5 1.6 subtract_convert_fusion.1
  95.1 0.6 fusion.28
  95.7 0.6 fusion.29
  96.3 1.0 fusion.1
  97.4 2.0 fusion.6
  99.4 1.1 copy.64
  100.5 2.7 fusion.12
  103.2 0.2 reduce-scatter.2.cloned.1.call-start
  103.5 81.0 %all-reduce.3.cloned.1.call-done = f32[512,2048]{1,0:T(8,128)} async-done(((f32[512,2048]{1,0:T(8,128)}), f32[512,2048]{1,0:T(8,128)}) %all-reduce.3.cloned.1.call-update) | async-done | bytes 4194320 | tf_op jit(solution)/shard_map/psum | solution.py:120
  184.4 2.7 multiply_reduce_fusion
  187.1 0.7 copy-done.3
  187.9 2.5 add_convert_fusion
  190.4 1.3 copy-done.4
  191.7 1.3 fusion.30
  192.9 7.2 %fusion.7 = f32[512,2048]{1,0:T(8,128)} fusion(bf16[512,2048]{1,0:T(8,128)(2,1)} %param.37, bf16[512,2048]{1,0:T(8,128)(2,1)} %copy-done.4, bf16[2048,512]{1,0:T(8,128)(2,1)} %param.36, f32[512,512]{1,0:T(8,128)S(1)} %fusion.30), kind=kOutput, calls=%fused_computation.22 | convolution fusion | flops 2149056512 | bytes 11534336 | tf_op jit(solution)/shard_map/dot_general | solution.py:129
  200.2 2.0 gather_fusion
  202.2 3.2 %bitcast_select_fusion = bf16[1,2,8,128,512]{4,3,1,0,2:T(8,128)(2,1)} fusion(bf16[8,2,128,512]{3,2,1,0:T(8,128)(2,1)} %gather_fusion, pred[8]{0:T(512)(128)(4,1)S(1)} %compare_and_fusion.2), kind=kLoop, calls=%fused_computation.12 | loop fusion | flops 1048576 | bytes 4194312 | tf_op jit(solution)/shard_map/jit(_take)/select_n | solution.py:63
  205.4 4.6 %all-to-all-start.2 = ((bf16[1,2,8,128,512]{4,3,1,0,2:T(8,128)(2,1)}), bf16[1,2,8,128,512]{4,3,1,0,2:T(8,128)(2,1)}, u32[]{:S(2)}, u32[]{:S(2)}) async-start(bf16[1,2,8,128,512]{4,3,1,0,2:T(8,128)(2,1)} %bitcast_select_fusion), calls=%async_computation.3 | async-start | bytes 4194304 | tf_op jit(solution)/shard_map/all_to_all | solution.py:64
  210.0 0.7 scatter_custom_fusion
  210.8 0.8 dynamic_slice.11
  211.5 40.2 %reduce-scatter.2.cloned.1.call-done = f32[512,256]{1,0:T(8,128)} async-done(((f32[512,2048]{1,0:T(8,128)}), f32[512,256]{1,0:T(8,128)}) %reduce-scatter.2.cloned.1.call-update) | async-done | bytes 524304 | tf_op jit(solution)/shard_map/reduce_scatter | solution.py:130
  251.8 1.2 multiply_reduce_fusion.1
  253.0 13.1 %psum.31 = f32[512]{0:T(512)S(1)} all-reduce(f32[512]{0:T(512)S(1)} %multiply_reduce_fusion.1), channel_id=1, replica_groups=mesh['req'=4,'head'=4,'blk'=2] {'head','blk'}, use_global_device_ids=true, to_apply=%region_11.14 | all-reduce | flops 512 | bytes 4096 | tf_op jit(solution)/shard_map/psum | solution.py:131
  266.1 1.3 add_convert_fusion.1
  267.3 1.0 copy.65
  268.3 4.2 %all-to-all-start.1 = ((bf16[2,256,256]{2,0,1:T(2,128)(2,1)}), bf16[2,256,256]{2,0,1:T(2,128)(2,1)S(1)}, u32[]{:S(2)}, u32[]{:S(2)}) async-start(bf16[2,256,256]{2,0,1:T(2,128)(2,1)} %copy.65), calls=%async_computation.2 | async-start | bytes 524288 | tf_op jit(solution)/shard_map/all_to_all | solution.py:31
  272.5 3.1 %copy.68 = bf16[1,2,2,4,128,512]{5,4,3,2,1,0:T(8,128)(2,1)} copy(bf16[1,2,2,4,128,512]{5,4,1,2,3,0:T(8,128)(2,1)} %bitcast.15) | data formatting | bytes 4194304 | tf_op jit(solution)/shard_map/all_to_all | solution.py:64
  275.6 5.1 %all-to-all-done.1 = bf16[2,256,256]{2,0,1:T(2,128)(2,1)S(1)} async-done(((bf16[2,256,256]{2,0,1:T(2,128)(2,1)}), bf16[2,256,256]{2,0,1:T(2,128)(2,1)S(1)}, u32[]{:S(2)}, u32[]{:S(2)}) %all-to-all-start.1) | async-done | bytes 262176 | tf_op jit(solution)/shard_map/all_to_all | solution.py:31
  280.8 0.6 gather_fusion.4
  281.3 0.8 broadcast_select_fusion
  (47 shorter events, 0.5 us)
Async XLA Ops:
  7.2 193.0 %copy-start = (bf16[1,2,8,128,512]{4,3,2,1,0:T(8,128)(2,1)S(1)}, bf16[1,2,8,128,512]{4,3,2,1,0:T(8,128)(2,1)}, u32[]{:S(2)}) copy-start(bf16[1,2,8,128,512]{4,3,2,1,0:T(8,128)(2,1)} %param.26) | copy-start | bytes 6291460
  7.2 19.0 %copy-start.12 = (s32[8]{0:T(128)S(1)}, s32[8]{0:T(128)}, u32[]{:S(2)}) copy-start(s32[8]{0:T(128)} %param.22) | copy-start | bytes 100
  7.2 19.0 %copy-start.1 = (s32[8]{0:T(128)S(1)}, s32[8]{0:T(128)}, u32[]{:S(2)}) copy-start(s32[8]{0:T(128)} %param.23) | copy-start | bytes 100
  7.2 19.7 %copy-start.2 = (s32[8]{0:T(128)S(1)}, s32[8]{0:T(128)}, u32[]{:S(2)}) copy-start(s32[8]{0:T(128)} %param.24) | copy-start | bytes 100
  7.2 46.3 %all-gather.2.cloned.1.call-start = ((), (), s32[]{:S(2)}) async-start(), calls=%async_computation.4 | async-start | bytes 2359296 | tf_op jit(solution)/shard_map/all_gather | solution.py:72
  8.1 0.7 copy-start.11
  26.1 158.3 %all-reduce.3.cloned.1.call-start = ((), (), s32[]{:S(2)}) async-start(), calls=%async_computation.5 | async-start | bytes 8388608 | tf_op jit(solution)/shard_map/psum | solution.py:120
  53.6 2.8 copy-start.6
  93.5 1.6 copy-start.5
  96.2 1.0 copy-start.8
  96.2 1.1 copy-start.9
  97.4 3.2 %copy-start.7 = (bf16[256,2048]{1,0:T(8,128)(2,1)S(1)}, bf16[256,2048]{1,0:T(8,128)(2,1)}, u32[]{:S(2)}) copy-start(bf16[256,2048]{1,0:T(8,128)(2,1)} %param.30) | copy-start | bytes 3145732
  103.2 83.9 %copy-start.10 = (f32[2048]{0:T(1024)S(1)}, f32[2048]{0:T(1024)}, u32[]{:S(2)}) copy-start(f32[2048]{0:T(1024)} %param.33) | copy-start | bytes 24580
  103.2 148.5 %reduce-scatter.2.cloned.1.call-start = ((), (), s32[]{:S(2)}) async-start(), calls=%async_computation.6 | async-start | bytes 4718592 | tf_op jit(solution)/shard_map/reduce_scatter | solution.py:130
  184.4 3.4 %copy-start.3 = (f32[512,2048]{1,0:T(8,128)S(1)}, f32[512,2048]{1,0:T(8,128)}, u32[]{:S(2)}) copy-start(f32[512,2048]{1,0:T(8,128)} %all-reduce.3.cloned.1.call-done) | copy-start | bytes 12582916
  187.9 3.8 %copy-start.13 = (bf16[2048,512]{1,0:T(8,128)(2,1)S(1)}, bf16[2048,512]{1,0:T(8,128)(2,1)}, u32[]{:S(2)}) copy-start(bf16[2048,512]{1,0:T(8,128)(2,1)} %param.35) | copy-start | bytes 6291460
  190.3 1.3 copy-start.4
  205.4 62.9 %all-to-all-start.2 = ((bf16[1,2,8,128,512]{4,3,1,0,2:T(8,128)(2,1)}), bf16[1,2,8,128,512]{4,3,1,0,2:T(8,128)(2,1)}, u32[]{:S(2)}, u32[]{:S(2)}) async-start(bf16[1,2,8,128,512]{4,3,1,0,2:T(8,128)(2,1)} %bitcast_select_fusion), calls=%async_computation.3 | async-start | bytes 4194304 | tf_op jit(solution)/shard_map/all_to_all | solution.py:64
  268.3 12.4 %all-to-all-start.1 = ((bf16[2,256,256]{2,0,1:T(2,128)(2,1)}), bf16[2,256,256]{2,0,1:T(2,128)(2,1)S(1)}, u32[]{:S(2)}, u32[]{:S(2)}) async-start(bf16[2,256,256]{2,0,1:T(2,128)(2,1)} %copy.65), calls=%async_computation.2 | async-start | bytes 524288 | tf_op jit(solution)/shard_map/all_to_all | solution.py:31
Sparse Core Ops, SparseCore 0:
  26.2 27.3 all-gather.1
  103.3 81.0 all-reduce.2
  200.3 51.3 reduce-scatter.1
where the time goes:
time: 290 us; the launch traced here: 289 us
  waiting for transfers between devices  147 us (51%)
  blocking collectives  41.2 us (14%)
  local copies, waits for them, and re-layouts  33.5 us (12%)
  matrix products  23.2 us (8%)
  other arithmetic  20.8 us (7%)
  between operations  14 us (5%)
  starting transfers between devices  9.1 us (3%)
    psum x1, waiting for transfers between devices, on_device(): totals = lax.psum(partial_value, ('head', 'blk'))  81 us
    reduce_scatter x1, waiting for transfers between devices, on_device(): lax.psum_scatter(down_sum, ('head', 'blk'), scatter_dimension=1, tiled=True)  40.2 us
    all_gather x1, waiting for transfers between devices, on_device(): full_x = lax.all_gather(local_x, ('head', 'blk'), axis=2, tiled=True)  20.6 us
    all_to_all x1, blocking collectives, on_device(): lax.all_to_all(jnp.take(group_rows, slot_request, axis=0), 'req', split_a...  15 us
    psum x1, blocking collectives, on_device(): lax.psum(jnp.sum(down_share * down_share, axis=-1), ('head', 'blk'))  13.1 us
    psum x1, blocking collectives, on_device(): lax.psum((jnp.sum(queries * queries, axis=-1), jnp.sum(keys_new * keys_ne...  13.1 us
    unnamed x33, local copies, waits for them, and re-layouts  9.4 us
    dot_general x1, matrix products, on_device(): down_sum = jnp.dot(inner, down_weight, preferred_element_type=jnp.float32)  7.24 us
  transfers between devices with their start and end apart: 5, of which 4 were waited for; matrix products, arithmetic and copies ran while one was open for 7% of the time, Pallas kernels for 0%

commit v1 on v0

v1 whole, which is shorter than its diff:
```python
import functools

import jax
import jax.numpy as jnp
from jax import lax
from jax.experimental import pallas as pl
from jax.experimental.pallas import tpu as pltpu
from jax.sharding import PartitionSpec as P

HD = 128


EPSILON = 1e-06
ROPE_BASE = 500000.0


BF = jnp.bfloat16
F32 = jnp.float32


def layer_kernel(
    dims,
    cached_ref, valid_ref, xt, ht, cos_ref, sin_ref, ac_hbm, wq, wk, wv, wo_hbm, wg, wu, wd_hbm,
    qg, kg, ag, mg,
    out, rel,
    xfull, wqkv, wo, wgu, wd, ac, qkv, stat_mine, stat_all, scale, qb, kb, vb, attended,
    acc, sb1, rb1, sc1, rc1, sb2, rb2, sc2, rc2, stfull, res,
    bsend, xz_recv, h_send, h_recv, lsem, xa_send, xa_recv, st_send, st_recv,
    r1_send, r1_recv, r2_send, r2_recv, sa_send, sa_recv, d1_send, d1_recv, d2_send, d2_recv,
    f_send, f_recv,
):
    nreq, nhead, slots, sc, tokens, tb, w, rows = dims
    model = w * nhead * 2
    rtot = sc * tokens
    r = lax.axis_index("req")
    h = lax.axis_index("head")
    b = lax.axis_index("blk")
    k = h * 2 + b
    other = 1 - b
    span = ht.shape[2]

    def dev(rr, hh, bb):
        return {"req": rr, "head": hh, "blk": bb}

    def rcopy(src, dst, ssem, rsem, rr, hh, bb):
        return pltpu.make_async_remote_copy(
            src_ref=src, dst_ref=dst, send_sem=ssem, recv_sem=rsem,
            device_id=dev(rr, hh, bb), device_id_type=pl.DeviceIdType.MESH,
        )

    barrier = pltpu.get_barrier_semaphore()

    def greet(rr, hh, bb):
        pl.semaphore_signal(
            barrier, inc=1, device_id=dev(rr, hh, bb), device_id_type=pl.DeviceIdType.MESH
        )

    def greet_z(i, carry):
        greet(lax.rem(r + i, nreq), h, b)
        return carry

    lax.fori_loop(1, nreq, greet_z, 0)
    for i in range(1, nhead * 2):
        kk = lax.rem(k + i, nhead * 2)
        greet(r, kk // 2, lax.rem(kk, 2))

    def greet_final(i, carry):
        m = i // nreq
        kk = m * (tokens // rows) + (r * tb) // rows
        rr = lax.rem(i, nreq)

        greet(rr, kk // 2, lax.rem(kk, 2))
        return carry

    lax.fori_loop(0, slots, greet_final, 0)
    first_row = k * rows
    my_slot = first_row // tokens
    my_off = lax.rem(first_row, tokens)
    base_req = my_off // tb
    n_dest = rows // tb
    own_dest = jnp.logical_and(base_req <= r, r < base_req + n_dest)
    locals_ = []

    def load(src, dst, i):
        c = pltpu.make_async_copy(src, dst, lsem.at[i])
        c.start()
        locals_.append(c)

    load(wq, wqkv.at[:, 0:w], 0)
    load(wk, wqkv.at[:, w : 2 * w], 1)
    load(wv, wqkv.at[:, 2 * w : 3 * w], 2)
    load(ac_hbm, ac, 3)
    load(wo_hbm, wo, 4)
    load(wg, wgu.at[:, 0 : wg.shape[1]], 5)
    load(wu, wgu.at[:, wg.shape[1] : 2 * wg.shape[1]], 6)
    load(wd_hbm, wd, 7)
    total = (nreq - 1) + (2 * nhead - 1) + slots
    pl.semaphore_wait(barrier, total)

    my_tok = pl.multiple_of(r * tb, tb)

    def send_x(i, carry):
        rr = lax.rem(r + i, nreq)
        rcopy(
            xt.at[pl.ds(rr * sc, sc)], xfull.at[k, :, pl.ds(my_tok, tb)],
            bsend, xz_recv, rr, h, b,
        ).start()
        return carry

    lax.fori_loop(1, nreq, send_x, 0)
    pltpu.make_async_copy(
        xt.at[pl.ds(r * sc, sc)], xfull.at[k, :, pl.ds(my_tok, tb)], xz_recv
    ).start()
    pltpu.make_async_copy(xfull.at[k], xfull.at[k], xz_recv).wait()

    def gather_send(full, ssem, rsem):
        for d in range(1, nhead):
            rcopy(full.at[k], full.at[k], ssem, rsem.at[k], r, lax.rem(h + d, nhead), b).start()
        rcopy(full.at[k], full.at[k], ssem, rsem.at[k], r, h, other).start()

    def got(full, rsem, kk):
        pltpu.make_async_copy(full.at[kk], full.at[kk], rsem.at[kk]).wait()

    def forward(full, ssem, rsem, d):
        kk = lax.rem(h + nhead - d, nhead) * 2 + b
        got(full, rsem, kk)
        rcopy(full.at[kk], full.at[kk], ssem, rsem.at[kk], r, h, other).start()

    gather_send(xfull, xa_send, xa_recv)

    my_pos = pl.multiple_of(r * span, span)

    def send_h(i, carry):
        rr = lax.rem(r + i, nreq)
        rcopy(
            ht.at[:, pl.ds(rr * sc, sc)], rel.at[:, :, pl.ds(my_pos, span)],
            h_send, h_recv, rr, h, b,
        ).start()
        return carry

    lax.fori_loop(1, nreq, send_h, 0)
    pltpu.make_async_copy(
        ht.at[:, pl.ds(r * sc, sc)], rel.at[:, :, pl.ds(my_pos, span)], h_recv
    ).start()

    for d in range(1, nhead):
        forward(xfull, xa_send, xa_recv, d)
    for d in range(nhead):
        got(xfull, xa_recv, lax.rem(h + nhead - d, nhead) * 2 + other)
    for c in locals_[:3]:
        c.wait()

    tile = 128
    per_slot = tokens // tile

    def project(i, carry):
        s = i // per_slot
        at = pl.multiple_of(lax.rem(i, per_slot) * tile, tile)
        here = pl.multiple_of(i * tile, tile)
        x = jnp.concatenate(
            [xfull[kk, s, pl.ds(at, tile), :] for kk in range(2 * nhead)], axis=1
        )
        y = jnp.dot(x, wqkv[...], preferred_element_type=F32)
        qkv[pl.ds(here, tile), :] = y
        q, kn = y[:, :w], y[:, w : 2 * w]
        lanes = lax.broadcasted_iota(jnp.int32, (tile, tile), 1)
        sums = jnp.where(
            lanes == 0,
            jnp.sum(q * q, axis=1, keepdims=True),
            jnp.where(lanes == 1, jnp.sum(kn * kn, axis=1, keepdims=True), 0.0),
        )
        stat_mine[i] = sums.T[0:8, :]
        return carry

    lax.fori_loop(0, rtot // tile, project, 0)
    for i in range(1, 2 * nhead):
        kk = lax.rem(k + i, 2 * nhead)
        rcopy(
            stat_mine, stat_all.at[k], st_send, st_recv.at[k], r, kk // 2, lax.rem(kk, 2)
        ).start()
    stat_all[k] = stat_mine[...]
    for i in range(1, 2 * nhead):
        kk = lax.rem(k + i, 2 * nhead)
        pltpu.make_async_copy(stat_all.at[kk], stat_all.at[kk], st_recv.at[kk]).wait()
    scale[...] = lax.rsqrt(jnp.sum(stat_all[...], axis=0) / model + EPSILON)

    heads_here = w // HD

    def finish(i, carry):
        here = pl.multiple_of(i * tile, tile)
        sq = jnp.concatenate([scale[i], jnp.zeros((tile - 8, tile), F32)], axis=0).T
        cosv = cos_ref[pl.ds(here, tile), :]
        sinv = sin_ref[pl.ds(here, tile), :]
        q = qkv[pl.ds(here, tile), 0:w] * sq[:, 0:1] * qg[...]
        kn = qkv[pl.ds(here, tile), w : 2 * w] * sq[:, 1:2] * kg[...]
        for hh in range(heads_here):
            cut = slice(hh * HD, (hh + 1) * HD)
            qh, kh = q[:, cut], kn[:, cut]
            qb[pl.ds(here, tile), cut] = (qh * cosv + pltpu.roll(qh, HD // 2, 1) * sinv).astype(BF)
            kb[pl.ds(here, tile), cut] = (kh * cosv + pltpu.roll(kh, HD // 2, 1) * sinv).astype(BF)
        vb[pl.ds(here, tile), :] = qkv[pl.ds(here, tile), 2 * w : 3 * w].astype(BF)
        return carry

    lax.fori_loop(0, rtot // tile, finish, 0)
    locals_[3].wait()
    score_scale = 1.0 / HD**0.5
    ctx = ac.shape[2]
    nt = (((1,), (1,)), ((), ()))

    def attend(i, carry):
        s = i // per_slot
        at = lax.rem(i, per_slot) * tile
        here = pl.multiple_of(i * tile, tile)
        there = pl.multiple_of(s * tokens, tokens)
        old_ok = lax.broadcasted_iota(jnp.int32, (tile, ctx), 1) < cached_ref[s]
        col = lax.broadcasted_iota(jnp.int32, (tile, tokens), 1)
        row = lax.broadcasted_iota(jnp.int32, (tile, tokens), 0) + at
        new_ok = jnp.logical_and(col <= row, col < valid_ref[s])
        for hh in range(heads_here):
            cut = slice(hh * HD, (hh + 1) * HD)
            q = qb[pl.ds(here, tile), cut]
            so = lax.dot_general(q, ac[0, s, :, cut], nt, preferred_element_type=F32) * score_scale
            sn = (
                lax.dot_general(q, kb[pl.ds(there, tokens), cut], nt, preferred_element_type=F32)
                * score_scale
            )
            so = jnp.where(old_ok, so, -1e30)
            sn = jnp.where(new_ok, sn, -1e30)
            top = jnp.maximum(
                jnp.max(so, axis=1, keepdims=True), jnp.max(sn, axis=1, keepdims=True)
            )
            po, pn = jnp.exp(so - top), jnp.exp(sn - top)
            inv = 1.0 / (jnp.sum(po, axis=1, keepdims=True) + jnp.sum(pn, axis=1, keepdims=True))
            o = jnp.dot(
                (po * inv).astype(BF), ac[1, s, :, cut], preferred_element_type=F32
            ) + jnp.dot(
                (pn * inv).astype(BF), vb[pl.ds(there, tokens), cut], preferred_element_type=F32
            )
            attended[pl.ds(here, tile), cut] = o.astype(BF)
        return carry

    lax.fori_loop(0, rtot // tile, attend, 0)
    locals_[4].wait()

    def pair_send(hh, p0, p1, sb, rb, ssem, rsem):
        mine = jnp.where(b == 0, p0, p1)
        theirs = jnp.where(b == 0, p1, p0)
        acc[hh] = mine
        sb[hh] = theirs.astype(BF)
        rcopy(sb.at[hh], rb.at[hh], ssem, rsem.at[hh], r, h, other).start()

    def chip_send(hh, d, rb, sc_, rc_, rsem, ssem2, rsem2):
        pltpu.make_async_copy(rb.at[hh], rb.at[hh], rsem.at[hh]).wait()
        total = acc[hh] + rb[hh].astype(F32)
        if d == 0:
            acc[hh] = total
        else:
            sc_[hh] = total.astype(BF)
            rcopy(sc_.at[hh], rc_.at[h], ssem2, rsem2.at[h], r, hh, b).start()

    def collect(rc_, rsem2):
        value = acc[h]
        for d in range(1, nhead):
            hh = lax.rem(h + nhead - d, nhead)
            pltpu.make_async_copy(rc_.at[hh], rc_.at[hh], rsem2.at[hh]).wait()
            value = value + rc_[hh].astype(F32)
        return value

    order = list(range(1, nhead)) + [0]
    for d in order:
        hh = lax.rem(h + d, nhead)
        at = pl.multiple_of(hh * 2 * rows, 2 * rows)
        p = jnp.dot(attended[pl.ds(at, 2 * rows), :], wo[...], preferred_element_type=F32)
        pair_send(hh, p[:rows], p[rows:], sb1, rb1, r1_send, r1_recv)
    for d in order:
        chip_send(lax.rem(h + d, nhead), d, rb1, sc1, rc1, r1_recv, r2_send, r2_recv)
    proj = collect(rc1, r2_recv)
    x_rows = jnp.concatenate(
        [xfull[kk, my_slot, pl.ds(pl.multiple_of(my_off, rows), rows), :] for kk in range(2 * nhead)],
        axis=1,
    ).astype(F32)
    norm = lax.rsqrt(jnp.mean(proj * proj, axis=1, keepdims=True) + EPSILON)
    stfull[k] = (x_rows + proj * norm * ag[...]).astype(BF)
    gather_send(stfull, sa_send, sa_recv)
    for c in locals_[5:]:
        c.wait()
    ff = wd.shape[0]

    def mlp(hh):
        s = jnp.concatenate([stfull[2 * hh], stfull[2 * hh + 1]], axis=0)
        gu = jnp.dot(s, wgu[...], preferred_element_type=F32)
        g, u = gu[:, :ff], gu[:, ff:]
        inner = (g * jax.nn.sigmoid(g) * u).astype(BF)
        p = jnp.dot(inner, wd[...], preferred_element_type=F32)
        pair_send(hh, p[:rows], p[rows:], sb2, rb2, d1_send, d1_recv)

    got(stfull, sa_recv, h * 2 + other)
    mlp(h)
    for d in range(1, nhead):
        forward(stfull, sa_send, sa_recv, d)
    for d in range(1, nhead):
        hh = lax.rem(h + nhead - d, nhead)
        got(stfull, sa_recv, hh * 2 + other)
        mlp(hh)
        chip_send(hh, d, rb2, sc2, rc2, d1_recv, d2_send, d2_recv)
    chip_send(h, 0, rb2, sc2, rc2, d1_recv, d2_send, d2_recv)
    down = collect(rc2, d2_recv)
    norm = lax.rsqrt(jnp.mean(down * down, axis=1, keepdims=True) + EPSILON)
    result = (stfull[k].astype(F32) + down * norm * mg[...]).astype(BF)
    for kk in range(2 * nhead):
        for i in range(n_dest):
            res[i, kk] = result[i * tb : (i + 1) * tb, kk * w : (kk + 1) * w]
    slot = r * sc + my_slot

    def send_home(i, carry):
        kk = lax.rem(k + i // n_dest, 2 * nhead)
        part = lax.rem(i, n_dest)
        rr = base_req + part
        mine = jnp.logical_and(rr == r, kk == k)

        @pl.when(mine)
        def _():
            c = pltpu.make_async_copy(res.at[part, kk], out.at[slot], f_recv)
            c.start()

        @pl.when(jnp.logical_not(mine))
        def _():
            rcopy(
                res.at[part, kk], out.at[slot], f_send, f_recv, rr, kk // 2, lax.rem(kk, 2)
            ).start()

        return carry

    lax.fori_loop(0, 2 * nhead * n_dest, send_home, 0)

    pltpu.make_async_copy(out, out, f_recv).wait()
    pltpu.make_async_copy(rel, rel, h_recv).wait()

    def drain(ref, sem):
        pltpu.make_async_copy(ref, ref, sem).wait()

    if nreq > 1:
        drain(xt.at[pl.ds(0, (nreq - 1) * sc)], bsend)
        drain(ht.at[:, pl.ds(0, (nreq - 1) * sc)], h_send)
    drain(xfull.at[pl.ds(0, 2 * nhead - 1)], xa_send)
    drain(stfull.at[pl.ds(0, 2 * nhead - 1)], sa_send)
    drain(stat_all.at[pl.ds(0, 2 * nhead - 1)], st_send)
    drain(sb1, r1_send)
    drain(sb2, d1_send)
    drain(sc1.at[pl.ds(0, nhead - 1)], r2_send)
    drain(sc2.at[pl.ds(0, nhead - 1)], d2_send)

    sent = res.shape[0] * res.shape[1]

    @pl.when(own_dest)
    def _():
        drain(out.at[pl.ds(0, sent - 1)], f_send)

    @pl.when(jnp.logical_not(own_dest))
    def _():
        drain(out.at[pl.ds(0, sent)], f_send)


def on_device(
    group_rows,
    slot_request,
    cache_len,
    group_len,
    attn_cache,
    hand_cache,
    query_weight,
    key_weight,
    value_weight,
    out_weight,
    query_gain,
    key_gain,
    attn_gain,
    mlp_gain,
    gate_weight,
    up_weight,
    down_weight,
):
    nreq = lax.axis_size("req")
    nhead = lax.axis_size("head")
    slots, tb, w = group_rows.shape
    sc = slots // nreq
    tokens = tb * nreq
    rows = sc * tokens // (2 * nhead)
    own_requests = lax.dynamic_slice_in_dim(slot_request, lax.axis_index("req") * sc, sc)
    cached = jnp.take(cache_len, own_requests)
    valid = jnp.take(group_len, own_requests)
    inverse = (
        jnp.zeros_like(slot_request).at[slot_request].set(jnp.arange(slots, dtype=jnp.int32))
    )
    xt = jnp.take(group_rows, slot_request, axis=0)
    ht = jnp.take(hand_cache[0], slot_request, axis=1)
    places = (cached[:, None] + jnp.arange(tokens, dtype=jnp.int32)[None, :]).reshape(-1)
    half = HD // 2
    frequency = ROPE_BASE ** (-(jnp.arange(half, dtype=F32) * 2.0 / HD))
    angles = places[:, None].astype(F32) * frequency
    cosv, sinv = jnp.cos(angles), jnp.sin(angles)
    cosv = jnp.concatenate([cosv, cosv], axis=1)
    sinv = jnp.concatenate([-sinv, sinv], axis=1)
    model = w * nhead * 2
    ff = gate_weight.shape[1]
    span = ht.shape[2]
    rtot = sc * tokens
    n8 = 2 * nhead
    dims = (nreq, nhead, slots, sc, tokens, tb, w, rows)
    dma = pltpu.SemaphoreType.DMA
    vm = pl.BlockSpec(memory_space=pltpu.VMEM)
    hb = pl.BlockSpec(memory_space=pl.ANY)
    sm = pl.BlockSpec(memory_space=pltpu.SMEM)
    blocks = lambda n: pltpu.VMEM((n, rows, model), BF)
    out, rel = pl.pallas_call(
        functools.partial(layer_kernel, dims),
        out_shape=(
            jax.ShapeDtypeStruct((slots, tb, w), BF),
            jax.ShapeDtypeStruct((ht.shape[0], sc, span * nreq, ht.shape[3]), BF),
        ),
        in_specs=[sm, sm, vm, hb, vm, vm, hb, hb, hb, hb, hb, hb, hb, hb, vm, vm, vm, vm],
        out_specs=(vm, hb),
        scratch_shapes=[
            pltpu.VMEM((n8, sc, tokens, w), BF),
            pltpu.VMEM((model, 3 * w), BF),
            pltpu.VMEM((w, model), BF),
            pltpu.VMEM((model, 2 * ff), BF),
            pltpu.VMEM((ff, model), BF),
            pltpu.VMEM(attn_cache.shape, BF),
            pltpu.VMEM((rtot, 3 * w), F32),
            pltpu.VMEM((rtot // 128, 8, 128), F32),
            pltpu.VMEM((n8, rtot // 128, 8, 128), F32),
            pltpu.VMEM((rtot // 128, 8, 128), F32),
            pltpu.VMEM((rtot, w), BF),
            pltpu.VMEM((rtot, w), BF),
            pltpu.VMEM((rtot, w), BF),
            pltpu.VMEM((rtot, w), BF),
            pltpu.VMEM((nhead, rows, model), F32),
            blocks(nhead), blocks(nhead), blocks(nhead), blocks(nhead),
            blocks(nhead), blocks(nhead), blocks(nhead), blocks(nhead),
            blocks(n8),
            pltpu.VMEM((rows // tb, n8, tb, w), BF),
            dma, dma, dma, dma, dma((8,)), dma, dma((n8,)), dma, dma((n8,)),
            dma, dma((nhead,)), dma, dma((nhead,)), dma, dma((n8,)),
            dma, dma((nhead,)), dma, dma((nhead,)),
            dma, dma,
        ],
        compiler_params=pltpu.CompilerParams(
            collective_id=0, has_side_effects=True, vmem_limit_bytes=56 * 1024 * 1024
        ),
    )(
        cached, valid, xt, ht, cosv, sinv, attn_cache, query_weight, key_weight, value_weight,
        out_weight, gate_weight, up_weight, down_weight,
        query_gain[None], key_gain[None], attn_gain[None], mlp_gain[None],
    )
    return (jnp.take(out, inverse, axis=0), rel[None])


def solution(mesh):
    in_specs = (
        P(None, "req", ("head", "blk")),
        P(),
        P(),
        P(),
        P(None, "req", None, ("head", "blk")),
        P("blk", None, None, "req", "head"),
        P(None, ("head", "blk")),
        P(None, ("head", "blk")),
        P(None, ("head", "blk")),
        P(("head", "blk"), None),
        P(("head", "blk")),
        P(("head", "blk")),
        P(),
        P(),
        P(None, ("head", "blk")),
        P(None, ("head", "blk")),
        P(("head", "blk"), None),
    )
    out_specs = (P(None, "req", ("head", "blk")), P("blk", None, "req", None, "head"))
    return jax.shard_map(
        on_device, mesh=mesh, in_specs=in_specs, out_specs=out_specs, check_vma=False
    )
```

time: 290 us -> 118 us (0.41)
  waiting for transfers between devices: 147 us -> 0 us
  Pallas kernels: 0 us -> 97.7 us
  blocking collectives: 41.2 us -> 0 us
  matrix products: 23.2 us -> 0 us
  local copies, waits for them, and re-layouts: 33.5 us -> 10.3 us
  between operations: 14 us -> 0.74 us
  other arithmetic: 20.8 us -> 9.12 us
  starting transfers between devices: 9.1 us -> 0 us
    pallas_call x0 -> x1, Pallas kernels: none -> 97.7 us  [on_device(): pl.pallas_call(functools.partial(layer_kernel, dims), out_shape=(jax.Shap...]
    psum x1 -> x0, waiting for transfers between devices: 81 us -> none  [on_device(): totals = lax.psum(partial_value, ('head', 'blk'))]
    reduce_scatter x1 -> x0, waiting for transfers between devices: 40.2 us -> none  [on_device(): lax.psum_scatter(down_sum, ('head', 'blk'), scatter_dimension=1, tiled=True)]
    psum x2 -> x0, blocking collectives: 26.2 us -> none  [the longest x1 13.1 us: on_device(): lax.psum(jnp.sum(down_share * down_share, axis=-1), ('head', 'blk'))]
    dot_general x9 -> x0, matrix products: 23.2 us -> none  [the longest x1 7.24 us: on_device(): down_sum = jnp.dot(inner, down_weight, preferred_element_type=jnp.float32)]
    all_gather x1 -> x0, waiting for transfers between devices: 20.6 us -> none  [on_device(): full_x = lax.all_gather(local_x, ('head', 'blk'), axis=2, tiled=True)]
    all_to_all x1 -> x0, blocking collectives: 15 us -> none  [on_device(): lax.all_to_all(jnp.take(group_rows, slot_request, axis=0), 'req', split_a...]
    all_to_all x2 -> x0, starting transfers between devices: 8.8 us -> none  [the longest x1 4.6 us: on_device(): lax.all_to_all(reordered, 'req', split_axis=2, concat_axis=3, tiled=True)]
  transfers between devices with their start and end apart: 5 -> 0, of which waited for: 4 -> 0; matrix products, arithmetic and copies ran while one was open for 7% -> 0% of each run, Pallas kernels for 0% -> 0%
where the time goes in v1:
time: 118 us
  Pallas kernels  97.7 us (83%)
  local copies, waits for them, and re-layouts  10.3 us (9%)
  other arithmetic  9.12 us (8%)
    pallas_call x1, Pallas kernels, on_device(): pl.pallas_call(functools.partial(layer_kernel, dims), out_shape=(jax.Shap...  97.7 us
    select_n x2, other arithmetic, on_device(): ht = jnp.take(hand_cache[0], slot_request, axis=1)  3.26 us
    unnamed x10, local copies, waits for them, and re-layouts  3.07 us

profile of v1, /device:TPU:0, one launch (start us, length us, event | category | flops | bytes accessed | tf_op | source)
XLA Modules:
  0.0 117.9 jit_solution(18297899091425378159)
XLA Ops:
  0.6 0.0 copy-start
  0.6 0.0 copy-start.3
  0.7 0.9 compare_select_fusion.1
  1.5 1.3 %gather_fusion.1 = s32[2]{0:T(128)S(1)} fusion(s32[8]{0:T(128)} %param.23, s32[1024]{0:T(1024)S(1)} %pad_clamp_fusion.2), kind=kCustom, calls=%fused_computation.clone | custom fusion | bytes 24 | tf_op jit(solution)/shard_map/jit(_take)/gather | solution.py:390
  2.8 1.3 %gather_fusion.2 = s32[2]{0:T(128)S(1)} fusion(s32[8]{0:T(128)} %param.24, s32[1024]{0:T(1024)S(1)} %pad_clamp_fusion.2), kind=kCustom, calls=%fused_computation.2.clone | custom fusion | bytes 24 | tf_op jit(solution)/shard_map/jit(_take)/gather | solution.py:391
  4.1 1.3 %broadcast_select_fusion.2 = (s32[2]{0:T(128)}, s32[2]{0:T(128)S(1)}) fusion(s32[2]{0:T(128)S(1)} %gather_fusion.2, s32[2]{0:T(128)S(1)} %gather_fusion.1, s32[8]{0:T(128)} %param.22, s32[]{:T(128)S(6)} %select_n.26), kind=kLoop, calls=%fused_computation.26 | loop fusion | flops 16 | bytes 44 | tf_op jit(solution)/shard_map/jit(_take)/select_n | solution.py:391
  5.4 0.0 copy-start.2
  5.4 0.1 convert_bitcast_fusion
  5.5 1.0 fusion.1
  6.5 1.0 pad_maximum_fusion
  7.5 0.0 copy-done.3
  7.5 0.0 copy-done
  7.5 2.0 %gather_fusion = bf16[8,2,128,512]{3,2,1,0:T(8,128)(2,1)} fusion(bf16[2,8,128,512]{3,2,1,0:T(8,128)(2,1)S(1)} %bitcast.11, s32[1024]{0:T(1024)S(1)} %pad_clamp_fusion.1), kind=kCustom, calls=%fused_computation.4 | custom fusion | bytes 4194336 | tf_op jit(solution)/shard_map/jit(_take)/gather | solution.py:396
  9.5 0.0 copy-done.2
  9.5 0.0 copy-start.1
  9.6 3.3 %fusion.ht = bf16[2,8,128,512]{3,2,1,0:T(8,128)(2,1)} fusion(bf16[8,2,128,512]{3,2,1,0:T(8,128)(2,1)} %gather_fusion, pred[8]{0:T(512)(128)(4,1)S(1)} %compare_and_fusion.1), kind=kLoop, calls=%fused_computation.7 | loop fusion | flops 1048576 | bytes 4194312 | tf_op jit(solution)/shard_map/jit(_take)/select_n | solution.py:396
  12.8 0.0 copy-done.1
  12.8 0.6 gather_fusion.3
  13.4 0.8 broadcast_select_fusion.1.xt
  14.2 97.7 %shard_map.176 = (bf16[8,64,256]{2,1,0:T(8,128)(2,1)}, bf16[2,2,512,512]{3,2,1,0:T(8,128)(2,1)}) custom-call(s32[2]{0:T(128)} %copy-done.2, s32[2]{0:T(128)} %get-tuple-element.11.valid_ref, bf16[8,64,256]{2,1,0:T(8,128)(2,1)} %broadcast_select_fusion.1.xt, bf16[2,8,128,512]{3,2,1,0:T(8,128)(2,1)} %fusion.ht, f32[512,128]{1,0:T(8,128)} %get-tuple-element.13.cos_ref, ...), custom_call_target="tpu_custom_call" | custom-call | tf_op jit(solution)/shard_map/pallas_call | solution.py:415
  111.9 0.6 scatter_custom_fusion
  112.5 1.5 %gather_fusion.4 = bf16[8,64,256]{2,1,0:T(8,128)(2,1)S(1)} fusion(bf16[8,64,256]{2,1,0:T(8,128)(2,1)} %get-tuple-element.6, s32[1024]{0:T(1024)S(1)} %pad_clamp_fusion), kind=kCustom, calls=%fused_computation.3.clone | custom fusion | bytes 524320 | tf_op jit(solution)/shard_map/jit(_take)/gather | solution.py:456
  114.1 0.8 broadcast_select_fusion
  114.9 3.0 %copy.25 = bf16[1,2,2,512,512]{4,3,2,1,0:T(8,128)(2,1)} copy(bf16[1,2,2,512,512]{4,3,2,1,0:T(8,128)(2,1)} %bitcast.12) | data formatting | bytes 4194304
  (10 shorter events, 0.1 us)
Async XLA Ops:
  0.6 6.9 %copy-start = (bf16[1,2,8,128,512]{4,3,2,1,0:T(8,128)(2,1)S(1)}, bf16[1,2,8,128,512]{4,3,2,1,0:T(8,128)(2,1)}, u32[]{:S(2)}) copy-start(bf16[1,2,8,128,512]{4,3,2,1,0:T(8,128)(2,1)} %param.26) | copy-start | bytes 6291460
  0.6 6.9 %copy-start.3 = (s32[8]{0:T(128)S(1)}, s32[8]{0:T(128)}, u32[]{:S(2)}) copy-start(s32[8]{0:T(128)} %param.22) | copy-start | bytes 100
  5.4 4.1 %copy-start.2 = (s32[2]{0:T(128)}, s32[2]{0:T(128)S(1)}, u32[]{:S(2)}) copy-start(s32[2]{0:T(128)S(1)} %get-tuple-element.12.cached_ref) | copy-start | bytes 28
  9.5 3.3 %copy-start.1 = (bf16[8,64,256]{2,1,0:T(8,128)(2,1)S(1)}, bf16[8,64,256]{2,1,0:T(8,128)(2,1)}, u32[]{:S(2)}) copy-start(bf16[8,64,256]{2,1,0:T(8,128)(2,1)} %param.21) | copy-start | bytes 786436

commit v2 on v1

--- a/solution.py
+++ b/solution.py
@@ -20,11 +20,11 @@
 
 def layer_kernel(
     dims,
-    cached_ref, valid_ref, xt, ht, cos_ref, sin_ref, ac_hbm, wq, wk, wv, wo_hbm, wg, wu, wd_hbm,
+    slot_ref, clen_ref, glen_ref, group, hand, freq, ac_hbm, wq, wk, wv, wo_hbm, wg, wu, wd_hbm,
     qg, kg, ag, mg,
-    out, rel,
+    landed, rel,
     xfull, wqkv, wo, wgu, wd, ac, qkv, stat_mine, stat_all, scale, qb, kb, vb, attended,
-    acc, sb1, rb1, sc1, rc1, sb2, rb2, sc2, rc2, stfull, res,
+    xt, ht_in, ht, cos_ref, sin_ref, acc, sb1, rb1, sc1, rc1, sb2, rb2, sc2, rc2, stfull, res,
     bsend, xz_recv, h_send, h_recv, lsem, xa_send, xa_recv, st_send, st_recv,
     r1_send, r1_recv, r2_send, r2_recv, sa_send, sa_recv, d1_send, d1_recv, d2_send, d2_recv,
     f_send, f_recv,
@@ -94,6 +94,13 @@
     load(wg, wgu.at[:, 0 : wg.shape[1]], 5)
     load(wu, wgu.at[:, wg.shape[1] : 2 * wg.shape[1]], 6)
     load(wd_hbm, wd, 7)
+    load(hand, ht_in, 8)
+
+    def order_x(i, carry):
+        xt[i] = group[slot_ref[i]]
+        return carry
+
+    lax.fori_loop(0, slots, order_x, 0)
     total = (nreq - 1) + (2 * nhead - 1) + slots
     pl.semaphore_wait(barrier, total)
 
@@ -129,6 +136,17 @@
     gather_send(xfull, xa_send, xa_recv)
 
     my_pos = pl.multiple_of(r * span, span)
+    locals_[8].wait()
+    step = min(span, 32)
+
+    def order_h(i, carry):
+        s = i // (span // step)
+        at = pl.multiple_of(lax.rem(i, span // step) * step, step)
+        for c in range(hand.shape[0]):
+            ht[c, s, pl.ds(at, step), :] = ht_in[c, slot_ref[s], pl.ds(at, step), :]
+        return carry
+
+    lax.fori_loop(0, slots * (span // step), order_h, 0)
 
     def send_h(i, carry):
         rr = lax.rem(r + i, nreq)
@@ -143,15 +161,31 @@
         ht.at[:, pl.ds(r * sc, sc)], rel.at[:, :, pl.ds(my_pos, span)], h_recv
     ).start()
 
+    half = HD // 2
+
+    def angles(i, carry):
+        here = pl.multiple_of(i * 128, 128)
+        s = i // (tokens // 128)
+        start = clen_ref[slot_ref[r * sc + s]] + lax.rem(i, tokens // 128) * 128
+        place = lax.broadcasted_iota(jnp.int32, (128, HD), 0) + start
+        lane = lax.broadcasted_iota(jnp.int32, (128, HD), 1)
+        angle = place.astype(F32) * freq[...]
+        cos_ref[pl.ds(here, 128), :] = jnp.cos(angle)
+        sine = jnp.sin(angle)
+        sin_ref[pl.ds(here, 128), :] = jnp.where(lane < half, -sine, sine)
+        return carry
+
+    lax.fori_loop(0, rtot // 128, angles, 0)
+
+    tile = 128
+    per_slot = tokens // tile
+
     for d in range(1, nhead):
         forward(xfull, xa_send, xa_recv, d)
     for d in range(nhead):
         got(xfull, xa_recv, lax.rem(h + nhead - d, nhead) * 2 + other)
     for c in locals_[:3]:
         c.wait()
-
-    tile = 128
-    per_slot = tokens // tile
 
     def project(i, carry):
         s = i // per_slot
@@ -212,10 +246,10 @@
         at = lax.rem(i, per_slot) * tile
         here = pl.multiple_of(i * tile, tile)
         there = pl.multiple_of(s * tokens, tokens)
-        old_ok = lax.broadcasted_iota(jnp.int32, (tile, ctx), 1) < cached_ref[s]
+        old_ok = lax.broadcasted_iota(jnp.int32, (tile, ctx), 1) < clen_ref[slot_ref[r * sc + s]]
         col = lax.broadcasted_iota(jnp.int32, (tile, tokens), 1)
         row = lax.broadcasted_iota(jnp.int32, (tile, tokens), 0) + at
-        new_ok = jnp.logical_and(col <= row, col < valid_ref[s])
+        new_ok = jnp.logical_and(col <= row, col < glen_ref[slot_ref[r * sc + s]])
         for hh in range(heads_here):
             cut = slice(hh * HD, (hh + 1) * HD)
             q = qb[pl.ds(here, tile), cut]
@@ -282,7 +316,7 @@
     norm = lax.rsqrt(jnp.mean(proj * proj, axis=1, keepdims=True) + EPSILON)
     stfull[k] = (x_rows + proj * norm * ag[...]).astype(BF)
     gather_send(stfull, sa_send, sa_recv)
-    for c in locals_[5:]:
+    for c in locals_[5:8]:
         c.wait()
     ff = wd.shape[0]
 
@@ -320,20 +354,20 @@
 
         @pl.when(mine)
         def _():
-            c = pltpu.make_async_copy(res.at[part, kk], out.at[slot], f_recv)
+            c = pltpu.make_async_copy(res.at[part, kk], landed.at[slot], f_recv)
             c.start()
 
         @pl.when(jnp.logical_not(mine))
         def _():
             rcopy(
-                res.at[part, kk], out.at[slot], f_send, f_recv, rr, kk // 2, lax.rem(kk, 2)
+                res.at[part, kk], landed.at[slot], f_send, f_recv, rr, kk // 2, lax.rem(kk, 2)
             ).start()
 
         return carry
 
     lax.fori_loop(0, 2 * nhead * n_dest, send_home, 0)
 
-    pltpu.make_async_copy(out, out, f_recv).wait()
+    pltpu.make_async_copy(landed, landed, f_recv).wait()
     pltpu.make_async_copy(rel, rel, h_recv).wait()
 
     def drain(ref, sem):
@@ -354,11 +388,19 @@
 
     @pl.when(own_dest)
     def _():
-        drain(out.at[pl.ds(0, sent - 1)], f_send)
+        drain(landed.at[pl.ds(0, sent - 1)], f_send)
 
     @pl.when(jnp.logical_not(own_dest))
     def _():
-        drain(out.at[pl.ds(0, sent)], f_send)
+        drain(landed.at[pl.ds(0, sent)], f_send)
+
+
+def home_kernel(slot_ref, landed, home):
+    def one(s, carry):
+        home[slot_ref[s]] = landed[s]
+        return carry
+
+    lax.fori_loop(0, landed.shape[0], one, 0)
 
 
 def on_device(
@@ -386,24 +428,13 @@
     sc = slots // nreq
     tokens = tb * nreq
     rows = sc * tokens // (2 * nhead)
-    own_requests = lax.dynamic_slice_in_dim(slot_request, lax.axis_index("req") * sc, sc)
-    cached = jnp.take(cache_len, own_requests)
-    valid = jnp.take(group_len, own_requests)
-    inverse = (
-        jnp.zeros_like(slot_request).at[slot_request].set(jnp.arange(slots, dtype=jnp.int32))
-    )
-    xt = jnp.take(group_rows, slot_request, axis=0)
-    ht = jnp.take(hand_cache[0], slot_request, axis=1)
-    places = (cached[:, None] + jnp.arange(tokens, dtype=jnp.int32)[None, :]).reshape(-1)
     half = HD // 2
     frequency = ROPE_BASE ** (-(jnp.arange(half, dtype=F32) * 2.0 / HD))
-    angles = places[:, None].astype(F32) * frequency
-    cosv, sinv = jnp.cos(angles), jnp.sin(angles)
-    cosv = jnp.concatenate([cosv, cosv], axis=1)
-    sinv = jnp.concatenate([-sinv, sinv], axis=1)
+    freq = jnp.concatenate([frequency, frequency])[None]
+    hand = hand_cache[0]
     model = w * nhead * 2
     ff = gate_weight.shape[1]
-    span = ht.shape[2]
+    span = hand.shape[2]
     rtot = sc * tokens
     n8 = 2 * nhead
     dims = (nreq, nhead, slots, sc, tokens, tb, w, rows)
@@ -412,13 +443,13 @@
     hb = pl.BlockSpec(memory_space=pl.ANY)
     sm = pl.BlockSpec(memory_space=pltpu.SMEM)
     blocks = lambda n: pltpu.VMEM((n, rows, model), BF)
-    out, rel = pl.pallas_call(
+    landed, rel = pl.pallas_call(
         functools.partial(layer_kernel, dims),
         out_shape=(
             jax.ShapeDtypeStruct((slots, tb, w), BF),
-            jax.ShapeDtypeStruct((ht.shape[0], sc, span * nreq, ht.shape[3]), BF),
+            jax.ShapeDtypeStruct((hand.shape[0], sc, span * nreq, hand.shape[3]), BF),
         ),
-        in_specs=[sm, sm, vm, hb, vm, vm, hb, hb, hb, hb, hb, hb, hb, hb, vm, vm, vm, vm],
+        in_specs=[sm, sm, sm, vm, hb, vm, hb, hb, hb, hb, hb, hb, hb, hb, vm, vm, vm, vm],
         out_specs=(vm, hb),
         scratch_shapes=[
             pltpu.VMEM((n8, sc, tokens, w), BF),
@@ -435,12 +466,17 @@
             pltpu.VMEM((rtot, w), BF),
             pltpu.VMEM((rtot, w), BF),
             pltpu.VMEM((rtot, w), BF),
+            pltpu.VMEM((slots, tb, w), BF),
+            pltpu.VMEM(hand.shape, BF),
+            pltpu.VMEM(hand.shape, BF),
+            pltpu.VMEM((rtot, HD), F32),
+            pltpu.VMEM((rtot, HD), F32),
             pltpu.VMEM((nhead, rows, model), F32),
             blocks(nhead), blocks(nhead), blocks(nhead), blocks(nhead),
             blocks(nhead), blocks(nhead), blocks(nhead), blocks(nhead),
             blocks(n8),
             pltpu.VMEM((rows // tb, n8, tb, w), BF),
-            dma, dma, dma, dma, dma((8,)), dma, dma((n8,)), dma, dma((n8,)),
+            dma, dma, dma, dma, dma((9,)), dma, dma((n8,)), dma, dma((n8,)),
             dma, dma((nhead,)), dma, dma((nhead,)), dma, dma((n8,)),
             dma, dma((nhead,)), dma, dma((nhead,)),
             dma, dma,
@@ -449,11 +485,17 @@
             collective_id=0, has_side_effects=True, vmem_limit_bytes=56 * 1024 * 1024
         ),
     )(
-        cached, valid, xt, ht, cosv, sinv, attn_cache, query_weight, key_weight, value_weight,
+        slot_request, cache_len, group_len, group_rows, hand, freq, attn_cache, query_weight, key_weight, value_weight,
         out_weight, gate_weight, up_weight, down_weight,
         query_gain[None], key_gain[None], attn_gain[None], mlp_gain[None],
     )
-    return (jnp.take(out, inverse, axis=0), rel[None])
+    home = pl.pallas_call(
+        home_kernel,
+        out_shape=jax.ShapeDtypeStruct((slots, tb, w), BF),
+        in_specs=[sm, vm],
+        out_specs=vm,
+    )(slot_request, landed)
+    return (home, rel[None])
 
 
 def solution(mesh):

time: 118 us -> 103 us (0.87)
  other arithmetic: 9.12 us -> 0.6 us
  local copies, waits for them, and re-layouts: 10.3 us -> 3.04 us
    select_n x7 -> x0, other arithmetic: 6.99 us -> none  [the longest x2 3.26 us: on_device(): ht = jnp.take(hand_cache[0], slot_request, axis=1)]
    gather x5 -> x0, local copies, waits for them, and re-layouts: 6.66 us -> none  [the longest x1 2 us: on_device(): ht = jnp.take(hand_cache[0], slot_request, axis=1)]
    pallas_call x0 -> x1, Pallas kernels: none -> 1.72 us  [on_device(): pl.pallas_call(home_kernel, out_shape=jax.ShapeDtypeStruct((slots, tb, w)...]
    pallas_call x1, Pallas kernels: 97.7 us -> 96.5 us  [on_device(): pl.pallas_call(functools.partial(layer_kernel, dims), out_shape=(jax.Shap...]
    unnamed x10 -> x1, local copies, waits for them, and re-layouts: 3.07 us -> 3.04 us
where the time goes in v2:
time: 103 us; the launch traced here: 102 us
  Pallas kernels  98.2 us (95%)
  local copies, waits for them, and re-layouts  3.04 us (3%)
    pallas_call x1, Pallas kernels, on_device(): pl.pallas_call(functools.partial(layer_kernel, dims), out_shape=(jax.Shap...  96.5 us
    unnamed x1, local copies, waits for them, and re-layouts  3.04 us

profile of v2, /device:TPU:0, one launch (start us, length us, event | category | flops | bytes accessed | tf_op | source)
XLA Modules:
  0.0 102.5 jit_solution(11070122215514328274)
XLA Ops:
  0.6 0.6 maximum_bitcast_fusion.freq
  1.2 96.5 %shard_map.176 = (bf16[8,64,256]{2,1,0:T(8,128)(2,1)}, bf16[2,2,512,512]{3,2,1,0:T(8,128)(2,1)}) custom-call(s32[8]{0:T(128)} %slot_ref.3, s32[8]{0:T(128)} %clen_ref.1, s32[8]{0:T(128)} %glen_ref.1, bf16[8,64,256]{2,1,0:T(8,128)(2,1)} %group.1, bf16[2,8,128,512]{3,2,1,0:T(8,128)(2,1)} %bitcast.8, f32[1,128]{1,0:T(1,128)} %maximum_bitcast_fusion.freq, ...), custom_call_target="tpu_custom_call" | custom-call | tf_op jit(solution)/shard_map/pallas_call | solution.py:446
  97.7 1.7 %shard_map.177 = bf16[8,64,256]{2,1,0:T(8,128)(2,1)} custom-call(s32[8]{0:T(128)} %slot_ref.3, bf16[8,64,256]{2,1,0:T(8,128)(2,1)} %get-tuple-element.4.landed), custom_call_target="tpu_custom_call" | custom-call | tf_op jit(solution)/shard_map/pallas_call | solution.py:492
  99.4 3.0 %copy.20 = bf16[1,2,2,512,512]{4,3,2,1,0:T(8,128)(2,1)} copy(bf16[1,2,2,512,512]{4,3,2,1,0:T(8,128)(2,1)} %bitcast.9) | data formatting | bytes 4194304
  (1 shorter events, 0.0 us)

commit v3 on v2

--- a/solution.py
+++ b/solution.py
@@ -273,7 +273,6 @@
             attended[pl.ds(here, tile), cut] = o.astype(BF)
         return carry
 
-    lax.fori_loop(0, rtot // tile, attend, 0)
     locals_[4].wait()
 
     def pair_send(hh, p0, p1, sb, rb, ssem, rsem):
@@ -304,10 +303,14 @@
     for d in order:
         hh = lax.rem(h + d, nhead)
         at = pl.multiple_of(hh * 2 * rows, 2 * rows)
+        for part in range(2 * rows // tile):
+            attend(hh * (2 * rows // tile) + part, 0)
         p = jnp.dot(attended[pl.ds(at, 2 * rows), :], wo[...], preferred_element_type=F32)
         pair_send(hh, p[:rows], p[rows:], sb1, rb1, r1_send, r1_recv)
-    for d in order:
-        chip_send(lax.rem(h + d, nhead), d, rb1, sc1, rc1, r1_recv, r2_send, r2_recv)
+        if d != 1:
+            before = d - 1 if d else nhead - 1
+            chip_send(lax.rem(h + before, nhead), before, rb1, sc1, rc1, r1_recv, r2_send, r2_recv)
+    chip_send(h, 0, rb1, sc1, rc1, r1_recv, r2_send, r2_recv)
     proj = collect(rc1, r2_recv)
     x_rows = jnp.concatenate(
         [xfull[kk, my_slot, pl.ds(pl.multiple_of(my_off, rows), rows), :] for kk in range(2 * nhead)],
@@ -395,12 +398,16 @@
         drain(landed.at[pl.ds(0, sent)], f_send)
 
 
-def home_kernel(slot_ref, landed, home):
+def home_kernel(slot_ref, landed, rel_in, home, rel_out):
+    rel_out[...] = rel_in[...]
+
     def one(s, carry):
         home[slot_ref[s]] = landed[s]
         return carry
 
-    lax.fori_loop(0, landed.shape[0], one, 0)
+    @pl.when(jnp.logical_and(pl.program_id(0) == 0, pl.program_id(1) == 0))
+    def _():
+        lax.fori_loop(0, landed.shape[0], one, 0)
 
 
 def on_device(
@@ -489,12 +496,17 @@
         out_weight, gate_weight, up_weight, down_weight,
         query_gain[None], key_gain[None], attn_gain[None], mlp_gain[None],
     )
-    home = pl.pallas_call(
+    part = pl.BlockSpec((1, 1) + rel.shape[2:], lambda i, j: (i, j, 0, 0))
+    home, rel = pl.pallas_call(
         home_kernel,
-        out_shape=jax.ShapeDtypeStruct((slots, tb, w), BF),
-        in_specs=[sm, vm],
-        out_specs=vm,
-    )(slot_request, landed)
+        grid=rel.shape[:2],
+        out_shape=(
+            jax.ShapeDtypeStruct((slots, tb, w), BF),
+            jax.ShapeDtypeStruct(rel.shape, BF),
+        ),
+        in_specs=[sm, pl.BlockSpec((slots, tb, w), lambda i, j: (0, 0, 0)), part],
+        out_specs=(pl.BlockSpec((slots, tb, w), lambda i, j: (0, 0, 0)), part),
+    )(slot_request, landed, rel)
     return (home, rel[None])
 
 

time: 103 us -> 101 us (0.981)
  local copies, waits for them, and re-layouts: 3.04 us -> 0 us
  Pallas kernels: 98.2 us -> 99.8 us
    unnamed x1 -> x0, local copies, waits for them, and re-layouts: 3.04 us -> none
    pallas_call x1, Pallas kernels: 1.72 us -> 4.03 us  [on_device(): pl.pallas_call(home_kernel, grid=rel.shape[:2], out_shape=(jax.ShapeDtype...]
where the time goes in v3:
time: 101 us
  Pallas kernels  99.8 us (99%)
    pallas_call x1, Pallas kernels, on_device(): pl.pallas_call(functools.partial(layer_kernel, dims), out_shape=(jax.Shap...  95.7 us
    pallas_call x1, Pallas kernels, on_device(): pl.pallas_call(home_kernel, grid=rel.shape[:2], out_shape=(jax.ShapeDtype...  4.03 us

profile of v3, /device:TPU:0, one launch (start us, length us, event | category | flops | bytes accessed | tf_op | source)
XLA Modules:
  0.0 101.0 jit_solution(6931576535934869329)
XLA Ops:
  0.6 0.6 maximum_bitcast_fusion.freq
  1.2 95.7 %shard_map.176 = (bf16[8,64,256]{2,1,0:T(8,128)(2,1)}, bf16[2,2,512,512]{3,2,1,0:T(8,128)(2,1)}) custom-call(s32[8]{0:T(128)} %slot_ref.3, s32[8]{0:T(128)} %clen_ref.1, s32[8]{0:T(128)} %glen_ref.1, bf16[8,64,256]{2,1,0:T(8,128)(2,1)} %group.1, bf16[2,8,128,512]{3,2,1,0:T(8,128)(2,1)} %bitcast.8, f32[1,128]{1,0:T(1,128)} %maximum_bitcast_fusion.freq, ...), custom_call_target="tpu_custom_call" | custom-call | tf_op jit(solution)/shard_map/pallas_call | solution.py:453
  97.0 4.0 %shard_map.177 = (bf16[8,64,256]{2,1,0:T(8,128)(2,1)}, bf16[2,2,512,512]{3,2,1,0:T(8,128)(2,1)}) custom-call(s32[8]{0:T(128)} %slot_ref.3, bf16[8,64,256]{2,1,0:T(8,128)(2,1)} %get-tuple-element.6.landed, bf16[2,2,512,512]{3,2,1,0:T(8,128)(2,1)} %get-tuple-element.7.rel_in), custom_call_target="tpu_custom_call" | custom-call | tf_op jit(solution)/shard_map/pallas_call | solution.py:500
  (1 shorter events, 0.0 us)
